TPU v7x, 512 devices: a whole 4x8x8 slice. The times are simulated.
512 devices in a mesh: blk: 32 (over y, x), head: 16 (over z, core).
Axes of the slice: x: 4, y: 8, z: 8, core: 2. Of those that a mesh axis runs over, the one named last changes fastest.
Arguments:
- tokens: bfloat16 [2048, 4096], P('blk', 'head'), may hold values from -6 to 6
- queries: bfloat16 [2048, 36864], P('blk', 'head'), may hold values from -600 to 600
- latents: bfloat16 [2048, 576], P('blk'), may hold values from -6 to 6
- value_up: bfloat16 [64, 512, 128], P('head'), may hold values from -0.25 to 0.25
- out_proj: bfloat16 [8192, 4096], P('head', 'blk'), may hold values from -0.09375 to 0.09375
- expert_ids: int32 [2048, 8], P('blk'), may hold values from 0 to 31, all different within a row; in each aligned block of 64 rows (0 to 63, 64 to 127, ...) at most 20 rows name the same one
- expert_gates: float32 [2048, 8], P('blk'), may hold values from 0.05 to 0.5
- w_gate: bfloat16 [32, 4096, 2048], P('blk', None, 'head'), may hold values from -0.09375 to 0.09375
- w_up: bfloat16 [32, 4096, 2048], P('blk', None, 'head'), may hold values from -0.09375 to 0.09375
- w_down: bfloat16 [32, 2048, 4096], P('blk', None, 'head'), may hold values from -0.125 to 0.125
Outputs:
- result: bfloat16 [2048, 4096], P('blk', 'head')
Inputs may be any that keep to these rules, and one draw needn't show every extreme that they name: `expert_ids`: among the tokens of one index of blk (aligned blocks of 64 rows) at most 20 choose one expert, and some expert is chosen by exactly 20 of them; the experts of one row differ.
All inputs are finite; a program needn't handle non-finite values.
Results may differ from a plain program's by a relative error of at most 0.013.
Values may be sent and summed in bfloat16 or wider, within the bound.
No kernel may reach another device: no remote copies, remote signals or barrier semaphores. Data moves between devices by JAX's collectives and lax.ppermute only.
A program may use at most 64 MiB of HBM per device.

v0:
```python
import jax
import jax.numpy as jnp
from jax import lax
from jax.sharding import PartitionSpec as P

D = 4096
LAT = 512
ROPE = 64
QKNOPE = 128
EXPERTS = 32
CAP = 20


def per_device(
    tokens, queries, latents, value_up, out_proj, expert_ids, expert_gates, w_gate, w_up, w_down
):
    row_count = tokens.shape[0]
    heads_here = value_up.shape[0]
    first_row = lax.axis_index("blk") * row_count
    score_scale = (QKNOPE + ROPE) ** (-0.5)
    query_heads = queries.reshape(row_count, heads_here, LAT + ROPE)
    query_pos = first_row + jnp.arange(row_count, dtype=jnp.int32)
    last_query = first_row + row_count - 1
    start_state = (
        jnp.full((row_count, heads_here), -1e30, jnp.float32),
        jnp.zeros((row_count, heads_here), jnp.float32),
        jnp.zeros((row_count, heads_here, LAT), jnp.float32),
    )
    segment = lax.all_gather(latents, "blk", axis=0, tiled=True)

    def compute(state_in):
        running_max, denominator, accumulated = state_in
        key_count = segment.shape[0]
        scores = (
            jnp.einsum("qhc,kc->qhk", query_heads, segment, preferred_element_type=jnp.float32)
            * score_scale
        )
        key_pos = jnp.arange(key_count, dtype=jnp.int32)
        allowed = (key_pos[None, :] <= query_pos[:, None])[:, None, :]
        scores = jnp.where(allowed, scores, -1e30)
        new_max = jnp.maximum(running_max, jnp.max(scores, axis=2))
        exp_weights = jnp.where(allowed, jnp.exp(scores - new_max[:, :, None]), 0.0)
        denominator = jnp.sum(exp_weights, axis=2)
        accumulated = jnp.einsum(
            "qhk,kc->qhc",
            exp_weights.astype(jnp.bfloat16),
            segment[:, :LAT],
            preferred_element_type=jnp.float32,
        )
        return (new_max, denominator, accumulated)

    def keep(state_in):
        return state_in

    running_max, denominator, accumulated = lax.cond(
        jnp.int32(0) <= last_query, compute, keep, start_state
    )
    context = (accumulated / denominator[:, :, None]).astype(jnp.bfloat16)
    lifted = jnp.einsum(
        "qhc,hcv->qhv", context, value_up, preferred_element_type=jnp.float32
    ).astype(jnp.bfloat16)
    lifted = lifted.reshape(row_count, heads_here * value_up.shape[2])
    partial_out = jnp.dot(
        lifted,
        lax.all_gather(out_proj, "blk", axis=1, tiled=True),
        preferred_element_type=jnp.float32,
    )
    attended = lax.psum_scatter(
        partial_out.astype(jnp.bfloat16), "head", scatter_dimension=1, tiled=True
    ).astype(jnp.float32)
    mid_state = (tokens.astype(jnp.float32) + attended).astype(jnp.bfloat16)
    mid_wide = mid_state.astype(jnp.float32)
    squares = lax.psum(jnp.sum(mid_wide * mid_wide, axis=1), "head")
    normed = (mid_wide * lax.rsqrt(squares / D + 1e-06)[:, None]).astype(jnp.bfloat16)
    flat_ids = expert_ids.reshape(-1)
    choose_count = expert_ids.shape[1]
    onehot_ids = (flat_ids[:, None] == jnp.arange(EXPERTS, dtype=jnp.int32)[None, :]).astype(
        jnp.int32
    )
    earlier = jnp.cumsum(onehot_ids, axis=0) - onehot_ids
    ranks = jnp.sum(earlier * onehot_ids, axis=1)
    slot_ids = flat_ids * CAP + ranks
    slot_hits = jnp.arange(EXPERTS * CAP, dtype=jnp.int32)[:, None] == slot_ids[None, :]
    select = jnp.sum(
        slot_hits.astype(jnp.bfloat16).reshape(EXPERTS * CAP, row_count, choose_count), axis=2
    )
    combine = jnp.sum(
        jnp.where(slot_hits, expert_gates.reshape(-1)[None, :], 0.0).reshape(
            EXPERTS * CAP, row_count, choose_count
        ),
        axis=2,
    )
    outgoing = (
        jnp.dot(select, normed, preferred_element_type=jnp.float32)
        .astype(jnp.bfloat16)
        .reshape(EXPERTS, CAP, normed.shape[1])
    )
    incoming = lax.all_to_all(outgoing, "blk", split_axis=0, concat_axis=1, tiled=True)
    contract_segment = lax.all_gather(incoming, "head", axis=2, tiled=True)
    gate_add = jnp.einsum(
        "esd,edf->esf", contract_segment, w_gate, preferred_element_type=jnp.float32
    )
    up_add = jnp.einsum("esd,edf->esf", contract_segment, w_up, preferred_element_type=jnp.float32)
    activation = (jax.nn.silu(gate_add) * up_add).astype(jnp.bfloat16)
    expert_out = jnp.einsum(
        "esf,efd->esd",
        lax.all_gather(activation, "head", axis=2, tiled=True),
        w_down,
        preferred_element_type=jnp.float32,
    ).astype(jnp.bfloat16)
    returned = lax.all_to_all(expert_out, "blk", split_axis=1, concat_axis=0, tiled=True)
    returned_wide = returned.reshape(EXPERTS * CAP, returned.shape[2]).astype(jnp.float32)
    routed = jnp.einsum("sr,sd->rd", combine, returned_wide, precision=lax.Precision.HIGHEST)
    return (mid_wide + routed).astype(jnp.bfloat16)


def solution(mesh):
    placed = (
        P("blk", "head"),
        P("blk", "head"),
        P("blk", None),
        P("head", None, None),
        P("head", "blk"),
        P("blk", None),
        P("blk", None),
        P("blk", None, "head"),
        P("blk", None, "head"),
        P("blk", None, "head"),
    )
    return jax.shard_map(
        per_device, mesh=mesh, in_specs=placed, out_specs=P("blk", "head"), check_vma=False
    )
```

profile of v0, /device:TPU:8, one launch (start us, length us, event | category | flops | bytes accessed | tf_op | source)
XLA Modules:
  0.0 443.7 jit_solution(13091606071966224623)
XLA Ops:
  6.5 0.7 all-gather.6.cloned.1.call-update
  7.3 0.0 all-gather.8.cloned.1.call-start
  7.3 0.7 all-gather.8.cloned.1.call-update
  8.0 0.0 reduce-scatter.2.cloned.1.call-start
  8.1 90.0 %all-gather.6.cloned.1.call-done = bf16[2048,576]{1,0:T(8,128)(2,1)} async-done(((bf16[64,576]{1,0:T(8,128)(2,1)}), bf16[2048,576]{1,0:T(8,128)(2,1)}) %all-gather.6.cloned.1.call-update) | async-done | bytes 2359312 | tf_op jit(solution)/shard_map/all_gather | solution.py:29
  98.1 6.0 %conditional.1 = (f32[64,4]{0,1:T(4,128)S(1)}, f32[64,4,512]{2,0,1:T(8,128)S(1)}) conditional(s32[]{:T(128)} %convert_element_type.66, () %tuple.13, (s32[]{:T(128)}, s32[64]{0:T(128)S(1)}, bf16[64,2304]{1,0:T(8,128)(2,1)}, bf16[2048,576]{1,0:T(8,128)(2,1)}) %tuple.14), branch_computations={%region_0.0_spmd, %region_1.4_spmd} | conditional | flops 1145700096 | bytes 22126384 | solution.py:55
  98.1 0.1 iota_compare_fusion
  98.2 1.4 reshape.109
  99.6 3.1 fusion.44
  102.7 0.8 fusion.2
  103.5 0.5 fusion.6
  104.0 0.3 fusion.25
  104.3 83.3 %all-gather.8.cloned.1.call-done = bf16[512,4096]{1,0:T(8,128)(2,1)} async-done(((bf16[512,128]{1,0:T(8,128)(2,1)}), bf16[512,4096]{1,0:T(8,128)(2,1)}) %all-gather.8.cloned.1.call-update) | async-done | bytes 4194320 | tf_op jit(solution)/shard_map/all_gather | solution.py:65
  187.6 3.8 convolution_convert_fusion
  191.5 0.0 all-gather.10.cloned.1.call-start
  191.6 0.1 copy.60
  191.7 0.1 eq.45
  191.8 0.1 eq.41
  191.9 1.2 reduce-window.6
  193.0 0.2 slice_reduce_fusion
  193.3 0.1 fusion.38
  193.4 0.1 reduce_sum.51
  193.5 0.1 copy.63
  193.6 0.1 copy.64
  193.7 0.5 fusion.30
  194.1 58.6 %reduce-scatter.2.cloned.1.call-done = bf16[64,256]{1,0:T(8,128)(2,1)} async-done(((bf16[64,4096]{1,0:T(8,128)(2,1)}), bf16[64,256]{1,0:T(8,128)(2,1)}) %reduce-scatter.2.cloned.1.call-update) | async-done | bytes 32784 | tf_op jit(solution)/shard_map/reduce_scatter | solution.py:68
  252.7 0.9 fusion.34
  253.6 23.6 %psum.7 = f32[64]{0:T(128)S(1)} all-reduce(f32[64]{0:T(128)S(1)} %fusion.34), channel_id=1, replica_groups=mesh['blk'=32,'head'=16] {'head'}, use_global_device_ids=true, to_apply=%region_11.12 | all-reduce | flops 64 | bytes 512 | tf_op jit(solution)/shard_map/psum | solution.py:73
  277.2 1.1 convolution_convert_fusion.2
  278.3 0.1 reshape.121
  278.3 24.3 %all_to_all.21 = bf16[32,20,256]{2,1,0:T(8,128)(2,1)S(1)} all-to-all(bf16[32,20,256]{2,1,0:T(8,128)(2,1)S(1)} %reshape.121), channel_id=1, replica_groups=mesh['blk'=32,'head'=16] {'blk'}, dimensions={0} | all-to-all | bytes 655360 | tf_op jit(solution)/shard_map/all_to_all | solution.py:98
  302.7 0.8 all_to_all.7
  303.5 0.0 all-gather.12.cloned.1.call-start
  303.6 49.1 %all-gather.10.cloned.1.call-done = bf16[1,640,4096]{2,1,0:T(8,128)(2,1)} async-done(((bf16[1,640,256]{2,1,0:T(8,128)(2,1)}), bf16[1,640,4096]{2,1,0:T(8,128)(2,1)}) %all-gather.10.cloned.1.call-update) | async-done | bytes 5242896 | tf_op jit(solution)/shard_map/all_gather | solution.py:99
  352.6 4.1 fusion.15
  356.8 3.4 fusion.22
  360.2 45.0 %all-gather.12.cloned.1.call-done = bf16[640,2048]{1,0:T(8,128)(2,1)} async-done(((bf16[640,128]{1,0:T(8,128)(2,1)}), bf16[640,2048]{1,0:T(8,128)(2,1)}) %all-gather.12.cloned.1.call-update) | async-done | bytes 2621456 | tf_op jit(solution)/shard_map/all_gather | solution.py:107
  405.3 2.6 fusion.18
  407.9 0.5 copy.86
  408.4 0.5 broadcast.62
  408.9 2.7 reduce.3
  411.6 0.8 reshape.133
  412.4 9.8 %all-to-all-start.1 = ((bf16[32,2,2560]{2,1,0:T(2,128)(2,1)}), bf16[32,2,2560]{2,1,0:T(2,128)(2,1)S(1)}, u32[]{:S(2)}, u32[]{:S(2)}) async-start(bf16[32,2,2560]{2,1,0:T(2,128)(2,1)} %reshape.133), calls=%async_computation.2 | async-start | bytes 655360 | tf_op jit(solution)/shard_map/all_to_all | solution.py:111
  422.3 0.1 copy.65
  422.3 0.5 select_reduce_fusion
  422.8 13.2 %all-to-all-done.1 = bf16[32,2,2560]{2,1,0:T(2,128)(2,1)S(1)} async-done(((bf16[32,2,2560]{2,1,0:T(2,128)(2,1)}), bf16[32,2,2560]{2,1,0:T(2,128)(2,1)S(1)}, u32[]{:S(2)}, u32[]{:S(2)}) %all-to-all-start.1) | async-done | bytes 327712 | tf_op jit(solution)/shard_map/all_to_all | solution.py:111
  436.0 0.3 reshape.134
  436.3 0.9 fusion.26
  (30 shorter events, 0.2 us)
Async XLA Ops:
  6.5 398.7 %copy-start = (bf16[1,2048,256]{2,1,0:T(8,128)(2,1)S(1)}, bf16[1,2048,256]{2,1,0:T(8,128)(2,1)}, u32[]{:S(2)}) copy-start(bf16[1,2048,256]{2,1,0:T(8,128)(2,1)} %param.21) | copy-start | bytes 3145732
  6.5 91.5 %all-gather.6.cloned.1.call-start = ((), (), s32[]{:S(2)}) async-start(), calls=%async_computation.3 | async-start | bytes 2703360 | tf_op jit(solution)/shard_map/all_gather | solution.py:29
  7.3 180.4 %all-gather.8.cloned.1.call-start = ((), (), s32[]{:S(2)}) async-start(), calls=%async_computation.4 | async-start | bytes 4325376 | tf_op jit(solution)/shard_map/all_gather | solution.py:65
  8.0 244.7 %reduce-scatter.2.cloned.1.call-start = ((), (), s32[]{:S(2)}) async-start(), calls=%async_computation.5 | async-start | bytes 557056 | tf_op jit(solution)/shard_map/reduce_scatter | solution.py:68
  98.1 6.0 %copy-start.8 = (bf16[4,512,128]{2,1,0:T(8,128)(2,1)S(1)}, bf16[4,512,128]{2,1,0:T(8,128)(2,1)}, u32[]{:S(2)}) copy-start(bf16[4,512,128]{2,1,0:T(8,128)(2,1)} %param.15) | copy-start | bytes 1572868
  99.6 3.1 copy-start.6
  104.3 87.3 %copy-start.3 = (s32[64,8]{0,1:T(8,128)S(1)}, s32[64,8]{0,1:T(8,128)}, u32[]{:S(2)}) copy-start(s32[64,8]{0,1:T(8,128)} %param.17) | copy-start | bytes 6148
  104.3 148.4 %copy-start.1 = (bf16[64,256]{1,0:T(8,128)(2,1)S(1)}, bf16[64,256]{1,0:T(8,128)(2,1)}, u32[]{:S(2)}) copy-start(bf16[64,256]{1,0:T(8,128)(2,1)} %param.12) | copy-start | bytes 98308
  191.5 161.1 %copy-start.7 = (bf16[1,4096,128]{2,1,0:T(8,128)(2,1)S(1)}, bf16[1,4096,128]{2,1,0:T(8,128)(2,1)}, u32[]{:S(2)}) copy-start(bf16[1,4096,128]{2,1,0:T(8,128)(2,1)} %param.19) | copy-start | bytes 3145732
  191.5 161.1 %all-gather.10.cloned.1.call-start = ((), (), s32[]{:S(2)}) async-start(), calls=%async_computation.6 | async-start | bytes 5570560 | tf_op jit(solution)/shard_map/all_gather | solution.py:99
  303.5 101.7 %all-gather.12.cloned.1.call-start = ((), (), s32[]{:S(2)}) async-start(), calls=%async_computation.7 | async-start | bytes 2785280 | tf_op jit(solution)/shard_map/all_gather | solution.py:107
  352.6 4.1 copy-start.5
  407.8 14.4 %copy-start.4 = (f32[64,8]{0,1:T(8,128)S(1)}, f32[64,8]{0,1:T(8,128)}, u32[]{:S(2)}) copy-start(f32[64,8]{0,1:T(8,128)} %param.18) | copy-start | bytes 6148
  407.9 28.5 %copy-start.2 = (bf16[64,256]{1,0:T(8,128)(2,1)S(1)}, bf16[64,256]{1,0:T(8,128)(2,1)}, u32[]{:S(2)}) copy-start(bf16[64,256]{1,0:T(8,128)(2,1)} %reduce-scatter.2.cloned.1.call-done) | copy-start | bytes 98308
  412.4 23.6 %all-to-all-start.1 = ((bf16[32,2,2560]{2,1,0:T(2,128)(2,1)}), bf16[32,2,2560]{2,1,0:T(2,128)(2,1)S(1)}, u32[]{:S(2)}, u32[]{:S(2)}) async-start(bf16[32,2,2560]{2,1,0:T(2,128)(2,1)} %reshape.133), calls=%async_computation.2 | async-start | bytes 655360 | tf_op jit(solution)/shard_map/all_to_all | solution.py:111
Sparse Core Ops, SparseCore 0:
  10.5 87.5 all-gather.5
  101.1 86.5 all-gather.7
  191.6 61.0 reduce-scatter.1
  303.6 48.9 all-gather.9
  360.3 44.8 all-gather.11
where the time goes:
time: 444 us
  waiting for transfers between devices  341 us (77%)
  blocking collectives  47.9 us (11%)
  matrix products  20.1 us (5%)
  between operations  13.3 us (3%)
  starting transfers between devices  10 us (2%)
  other arithmetic  6.52 us (1%)
  local copies, waits for them, and re-layouts  5.17 us (1%)
    all_gather x1, waiting for transfers between devices, per_device(): segment = lax.all_gather(latents, 'blk', axis=0, tiled=True)  90 us
    all_gather x1, waiting for transfers between devices, per_device(): lax.all_gather(out_proj, 'blk', axis=1, tiled=True)  83.3 us
    reduce_scatter x1, waiting for transfers between devices, per_device(): lax.psum_scatter(partial_out.astype(jnp.bfloat16), 'head', scatter_dimens...  58.6 us
    all_gather x1, waiting for transfers between devices, per_device(): contract_segment = lax.all_gather(incoming, 'head', axis=2, tiled=True)  49.1 us
    all_gather x1, waiting for transfers between devices, per_device(): lax.all_gather(activation, 'head', axis=2, tiled=True)  45 us
    all_to_all x1, blocking collectives, per_device(): lax.all_to_all(outgoing, 'blk', split_axis=0, concat_axis=1, tiled=True)  24.3 us
    psum x1, blocking collectives, per_device(): squares = lax.psum(jnp.sum(mid_wide * mid_wide, axis=1), 'head')  23.6 us
    all_to_all x1, waiting for transfers between devices, per_device(): lax.all_to_all(expert_out, 'blk', split_axis=1, concat_axis=0, tiled=True)  13.2 us
  transfers between devices with their start and end apart: 6, of which 6 were waited for; matrix products, arithmetic and copies ran while one was open for 2% of the time, Pallas kernels for 0%

commit v1 on v0

--- a/solution.py
+++ b/solution.py
@@ -26,7 +26,8 @@
         jnp.zeros((row_count, heads_here), jnp.float32),
         jnp.zeros((row_count, heads_here, LAT), jnp.float32),
     )
-    segment = lax.all_gather(latents, "blk", axis=0, tiled=True)
+    sent = jnp.stack([latents] * lax.axis_size("blk"))
+    segment = jnp.concatenate(lax.all_to_all(sent, "blk", 0, 0), axis=0)
 
     def compute(state_in):
         running_max, denominator, accumulated = state_in

time: 444 us -> 382 us (0.86)
  waiting for transfers between devices: 341 us -> 264 us
  starting transfers between devices: 10 us -> 20.5 us
    all_gather x1 -> x0, waiting for transfers between devices: 90 us -> none  [per_device(): segment = lax.all_gather(latents, 'blk', axis=0, tiled=True)]
    all_to_all x0 -> x1, waiting for transfers between devices: none -> 65.8 us  [per_device(): segment = jnp.concatenate(lax.all_to_all(sent, 'blk', 0, 0), axis=0)]
    all_gather x1, waiting for transfers between devices: 83.3 us -> 31.9 us  [per_device(): lax.all_gather(out_proj, 'blk', axis=1, tiled=True)]
    all_to_all x0 -> x1, starting transfers between devices: none -> 10.3 us  [per_device(): segment = jnp.concatenate(lax.all_to_all(sent, 'blk', 0, 0), axis=0)]
  transfers between devices with their start and end apart: 6 -> 6, of which waited for: 6 -> 6; matrix products, arithmetic and copies ran while one was open for 2% -> 3% of each run, Pallas kernels for 0% -> 0%
where the time goes in v1:
time: 382 us; the launch traced here: 381 us
  waiting for transfers between devices  264 us (69%)
  blocking collectives  47.9 us (13%)
  matrix products  21.6 us (6%)
  starting transfers between devices  20.5 us (5%)
  between operations  13.3 us (3%)
  local copies, waits for them, and re-layouts  7 us (2%)
  other arithmetic  6.51 us (2%)
    all_to_all x1, waiting for transfers between devices, per_device(): segment = jnp.concatenate(lax.all_to_all(sent, 'blk', 0, 0), axis=0)  65.8 us
    reduce_scatter x1, waiting for transfers between devices, per_device(): lax.psum_scatter(partial_out.astype(jnp.bfloat16), 'head', scatter_dimens...  58.8 us
    all_gather x1, waiting for transfers between devices, per_device(): contract_segment = lax.all_gather(incoming, 'head', axis=2, tiled=True)  48.7 us
    all_gather x1, waiting for transfers between devices, per_device(): lax.all_gather(activation, 'head', axis=2, tiled=True)  45 us
    all_gather x1, waiting for transfers between devices, per_device(): lax.all_gather(out_proj, 'blk', axis=1, tiled=True)  31.9 us
    all_to_all x1, blocking collectives, per_device(): lax.all_to_all(outgoing, 'blk', split_axis=0, concat_axis=1, tiled=True)  24.3 us
    psum x1, blocking collectives, per_device(): squares = lax.psum(jnp.sum(mid_wide * mid_wide, axis=1), 'head')  23.6 us
    all_to_all x1, waiting for transfers between devices, per_device(): lax.all_to_all(expert_out, 'blk', split_axis=1, concat_axis=0, tiled=True)  13.2 us
  transfers between devices with their start and end apart: 6, of which 6 were waited for; matrix products, arithmetic and copies ran while one was open for 3% of the time, Pallas kernels for 0%

profile of v1, /device:TPU:8, one launch (start us, length us, event | category | flops | bytes accessed | tf_op | source)
XLA Modules:
  0.0 381.0 jit_solution(10287543382940387727)
XLA Ops:
  6.5 0.7 all-gather.5.cloned.1.call-update
  7.3 2.8 stack.2
  10.0 10.3 %all-to-all-start = ((bf16[32,64,576]{2,1,0:T(8,128)(2,1)}), bf16[32,64,576]{2,1,0:T(8,128)(2,1)}, u32[]{:S(2)}, u32[]{:S(2)}) async-start(bf16[32,64,576]{2,1,0:T(8,128)(2,1)} %stack.2), calls=%async_computation | async-start | bytes 5242880 | tf_op jit(solution)/shard_map/all_to_all | solution.py:30
  20.4 0.0 reduce-scatter.2.cloned.1.call-start
  20.5 65.8 %all-to-all-done = bf16[32,64,576]{2,1,0:T(8,128)(2,1)} async-done(((bf16[32,64,576]{2,1,0:T(8,128)(2,1)}), bf16[32,64,576]{2,1,0:T(8,128)(2,1)}, u32[]{:S(2)}, u32[]{:S(2)}) %all-to-all-start) | async-done | bytes 2359328 | tf_op jit(solution)/shard_map/all_to_all | solution.py:30
  86.3 6.5 %conditional.1 = (f32[64,4]{0,1:T(4,128)S(1)}, f32[64,4,512]{2,0,1:T(8,128)S(1)}) conditional(s32[]{:T(128)} %convert_element_type.66, () %tuple.13, (s32[]{:T(128)}, s32[64]{0:T(128)S(1)}, bf16[64,2304]{1,0:T(8,128)(2,1)S(1)}, bf16[32,64,576]{2,1,0:T(8,128)(2,1)}) %tuple.26), branch_computations={%region_0.0_spmd, %region_1.4_spmd} | conditional | flops 1145700096 | bytes 12688148 | solution.py:56
  86.3 0.1 iota_compare_fusion
  86.4 0.4 reshape.114
  86.8 2.9 fusion.41
  89.7 2.4 fusion.1
  92.2 0.5 fusion.3
  92.7 0.3 fusion.22
  93.0 31.9 %all-gather.5.cloned.1.call-done = bf16[512,4096]{1,0:T(8,128)(2,1)} async-done(((bf16[512,128]{1,0:T(8,128)(2,1)}), bf16[512,4096]{1,0:T(8,128)(2,1)}) %all-gather.5.cloned.1.call-update) | async-done | bytes 4194320 | tf_op jit(solution)/shard_map/all_gather | solution.py:66
  124.9 3.8 %convolution_convert_fusion = bf16[64,4096]{1,0:T(8,128)(2,1)} fusion(bf16[512,4096]{1,0:T(8,128)(2,1)} %all-gather.5.cloned.1.call-done, bf16[4,8,8,128]{3,2,1,0:T(8,128)(2,1)S(1)} %fusion.22), kind=kOutput, calls=%fused_computation.19 | convolution fusion | flops 268697600 | bytes 4784128 | tf_op jit(solution)/shard_map/dot_general | solution.py:64
  128.7 0.0 all-gather.7.cloned.1.call-start
  128.8 0.1 copy.60
  128.9 0.1 eq.45
  129.0 0.1 eq.41
  129.1 1.2 reduce-window.6
  130.3 0.2 slice_reduce_fusion
  130.5 0.1 fusion.35
  130.6 0.1 reduce_sum.51
  130.7 0.1 copy.63
  130.8 0.1 copy.64
  130.9 0.5 fusion.27
  131.4 58.8 %reduce-scatter.2.cloned.1.call-done = bf16[64,256]{1,0:T(8,128)(2,1)} async-done(((bf16[64,4096]{1,0:T(8,128)(2,1)}), bf16[64,256]{1,0:T(8,128)(2,1)}) %reduce-scatter.2.cloned.1.call-update) | async-done | bytes 32784 | tf_op jit(solution)/shard_map/reduce_scatter | solution.py:69
  190.2 0.9 fusion.31
  191.1 23.6 %psum.7 = f32[64]{0:T(128)S(1)} all-reduce(f32[64]{0:T(128)S(1)} %fusion.31), channel_id=1, replica_groups=mesh['blk'=32,'head'=16] {'head'}, use_global_device_ids=true, to_apply=%region_11.12 | all-reduce | flops 64 | bytes 512 | tf_op jit(solution)/shard_map/psum | solution.py:74
  214.7 1.1 convolution_convert_fusion.2
  215.7 0.1 reshape.127
  215.8 24.3 %all_to_all.26 = bf16[32,20,256]{2,1,0:T(8,128)(2,1)S(1)} all-to-all(bf16[32,20,256]{2,1,0:T(8,128)(2,1)S(1)} %reshape.127), channel_id=1, replica_groups=mesh['blk'=32,'head'=16] {'blk'}, dimensions={0} | all-to-all | bytes 655360 | tf_op jit(solution)/shard_map/all_to_all | solution.py:99
  240.2 0.8 all_to_all.10
  241.0 0.2 all-gather.9.cloned.1.call-start
  241.2 48.7 %all-gather.7.cloned.1.call-done = bf16[1,640,4096]{2,1,0:T(8,128)(2,1)} async-done(((bf16[1,640,256]{2,1,0:T(8,128)(2,1)}), bf16[1,640,4096]{2,1,0:T(8,128)(2,1)}) %all-gather.7.cloned.1.call-update) | async-done | bytes 5242896 | tf_op jit(solution)/shard_map/all_gather | solution.py:100
  289.9 4.1 %fusion.12 = f32[640,128]{1,0:T(8,128)S(1)} fusion(bf16[1,640,4096]{2,1,0:T(8,128)(2,1)} %all-gather.7.cloned.1.call-done, bf16[1,4096,128]{2,1,0:T(8,128)(2,1)S(1)} %copy-done.7), kind=kOutput, calls=%fused_computation.17 | convolution fusion | flops 671088640 | bytes 6619136 | tf_op jit(solution)/shard_map/esd,edf->esf/dot_general | solution.py:101
  294.1 3.4 fusion.19
  297.5 45.0 %all-gather.9.cloned.1.call-done = bf16[640,2048]{1,0:T(8,128)(2,1)} async-done(((bf16[640,128]{1,0:T(8,128)(2,1)}), bf16[640,2048]{1,0:T(8,128)(2,1)}) %all-gather.9.cloned.1.call-update) | async-done | bytes 2621456 | tf_op jit(solution)/shard_map/all_gather | solution.py:108
  342.5 2.6 fusion.15
  345.1 0.5 copy.86
  345.6 0.5 broadcast.64
  346.2 2.7 reduce.3
  348.9 0.8 reshape.139
  349.7 9.8 %all-to-all-start.2 = ((bf16[32,2,2560]{2,1,0:T(2,128)(2,1)}), bf16[32,2,2560]{2,1,0:T(2,128)(2,1)S(1)}, u32[]{:S(2)}, u32[]{:S(2)}) async-start(bf16[32,2,2560]{2,1,0:T(2,128)(2,1)} %reshape.139), calls=%async_computation.3 | async-start | bytes 655360 | tf_op jit(solution)/shard_map/all_to_all | solution.py:112
  359.5 0.1 copy.65
  359.6 0.5 select_reduce_fusion
  360.1 13.2 %all-to-all-done.2 = bf16[32,2,2560]{2,1,0:T(2,128)(2,1)S(1)} async-done(((bf16[32,2,2560]{2,1,0:T(2,128)(2,1)}), bf16[32,2,2560]{2,1,0:T(2,128)(2,1)S(1)}, u32[]{:S(2)}, u32[]{:S(2)}) %all-to-all-start.2) | async-done | bytes 327712 | tf_op jit(solution)/shard_map/all_to_all | solution.py:112
  373.3 0.3 reshape.140
  373.6 0.9 fusion.23
  (30 shorter events, 0.2 us)
Async XLA Ops:
  6.5 336.0 %copy-start = (bf16[1,2048,256]{2,1,0:T(8,128)(2,1)S(1)}, bf16[1,2048,256]{2,1,0:T(8,128)(2,1)}, u32[]{:S(2)}) copy-start(bf16[1,2048,256]{2,1,0:T(8,128)(2,1)} %param.21) | copy-start | bytes 3145732
  6.5 118.4 %all-gather.5.cloned.1.call-start = ((), (), s32[]{:S(2)}) async-start(), calls=%async_computation.4 | async-start | bytes 4325376 | tf_op jit(solution)/shard_map/all_gather | solution.py:66
  10.0 76.2 %copy-start.3 = (bf16[64,2304]{1,0:T(8,128)(2,1)S(1)}, bf16[64,2304]{1,0:T(8,128)(2,1)}, u32[]{:S(2)}) copy-start(bf16[64,2304]{1,0:T(8,128)(2,1)} %param.13) | copy-start | bytes 884740
  10.0 76.2 %all-to-all-start = ((bf16[32,64,576]{2,1,0:T(8,128)(2,1)}), bf16[32,64,576]{2,1,0:T(8,128)(2,1)}, u32[]{:S(2)}, u32[]{:S(2)}) async-start(bf16[32,64,576]{2,1,0:T(8,128)(2,1)} %stack.2), calls=%async_computation | async-start | bytes 5242880 | tf_op jit(solution)/shard_map/all_to_all | solution.py:30
  20.4 169.8 %reduce-scatter.2.cloned.1.call-start = ((), (), s32[]{:S(2)}) async-start(), calls=%async_computation.5 | async-start | bytes 557056 | tf_op jit(solution)/shard_map/reduce_scatter | solution.py:69
  86.3 6.5 %copy-start.8 = (bf16[4,512,128]{2,1,0:T(8,128)(2,1)S(1)}, bf16[4,512,128]{2,1,0:T(8,128)(2,1)}, u32[]{:S(2)}) copy-start(bf16[4,512,128]{2,1,0:T(8,128)(2,1)} %param.15) | copy-start | bytes 1572868
  93.0 35.8 %copy-start.4 = (s32[64,8]{0,1:T(8,128)S(1)}, s32[64,8]{0,1:T(8,128)}, u32[]{:S(2)}) copy-start(s32[64,8]{0,1:T(8,128)} %param.17) | copy-start | bytes 6148
  93.0 97.2 %copy-start.1 = (bf16[64,256]{1,0:T(8,128)(2,1)S(1)}, bf16[64,256]{1,0:T(8,128)(2,1)}, u32[]{:S(2)}) copy-start(bf16[64,256]{1,0:T(8,128)(2,1)} %param.12) | copy-start | bytes 98308
  128.7 161.2 %copy-start.7 = (bf16[1,4096,128]{2,1,0:T(8,128)(2,1)S(1)}, bf16[1,4096,128]{2,1,0:T(8,128)(2,1)}, u32[]{:S(2)}) copy-start(bf16[1,4096,128]{2,1,0:T(8,128)(2,1)} %param.19) | copy-start | bytes 3145732
  128.7 161.2 %all-gather.7.cloned.1.call-start = ((), (), s32[]{:S(2)}) async-start(), calls=%async_computation.6 | async-start | bytes 5570560 | tf_op jit(solution)/shard_map/all_gather | solution.py:100
  241.0 101.5 %all-gather.9.cloned.1.call-start = ((), (), s32[]{:S(2)}) async-start(), calls=%async_computation.7 | async-start | bytes 2785280 | tf_op jit(solution)/shard_map/all_gather | solution.py:108
  289.9 4.1 %copy-start.6 = (bf16[1,640,4096]{2,1,0:T(8,128)(2,1)S(1)}, bf16[1,640,4096]{2,1,0:T(8,128)(2,1)}, u32[]{:S(2)}) copy-start(bf16[1,640,4096]{2,1,0:T(8,128)(2,1)} %all-gather.7.cloned.1.call-done) | copy-start | bytes 15728644
  345.1 14.4 %copy-start.5 = (f32[64,8]{0,1:T(8,128)S(1)}, f32[64,8]{0,1:T(8,128)}, u32[]{:S(2)}) copy-start(f32[64,8]{0,1:T(8,128)} %param.18) | copy-start | bytes 6148
  345.1 28.5 %copy-start.2 = (bf16[64,256]{1,0:T(8,128)(2,1)S(1)}, bf16[64,256]{1,0:T(8,128)(2,1)}, u32[]{:S(2)}) copy-start(bf16[64,256]{1,0:T(8,128)(2,1)} %reduce-scatter.2.cloned.1.call-done) | copy-start | bytes 98308
  349.7 23.6 %all-to-all-start.2 = ((bf16[32,2,2560]{2,1,0:T(2,128)(2,1)}), bf16[32,2,2560]{2,1,0:T(2,128)(2,1)S(1)}, u32[]{:S(2)}, u32[]{:S(2)}) async-start(bf16[32,2,2560]{2,1,0:T(2,128)(2,1)} %reshape.139), calls=%async_computation.3 | async-start | bytes 655360 | tf_op jit(solution)/shard_map/all_to_all | solution.py:112
Sparse Core Ops, SparseCore 0:
  10.4 114.4 all-gather.4
  128.9 61.2 reduce-scatter.1
  241.1 48.7 all-gather.6
  297.6 44.8 all-gather.8
